TPU v7x, 32 devices: a whole 2x2x4 slice. The times are simulated.
32 devices in a mesh: wide: 16 (over z, x, core), narrow: 2 (over y).
Axes of the slice: x: 2, y: 2, z: 4, core: 2. Of those that a mesh axis runs over, the one named last changes fastest.
Arguments:
- hess_inverse: bfloat16 [26880, 26880], P('wide', 'narrow'), may hold values from -0.0390625 to 0.0390625
- observations: bfloat16 [16, 26880], P('wide', 'narrow'), may hold values from -6 to 6
- adjoint_maps: bfloat16 [210, 2, 6144, 128], P('narrow', None, 'wide'), may hold values from -0.375 to 0.375
Outputs:
- estimate: float32 [6144, 210, 16], P(('wide', 'narrow'))
All inputs are finite; a program needn't handle non-finite values.
Results may differ from a plain program's by a relative error of at most 0.004.
Values may be sent and summed in bfloat16 or wider, within the bound.
A program may use at most 128 MiB of HBM per device.

v0:
```python
import math

import jax
import jax.numpy as jnp
from jax import lax
from jax.sharding import PartitionSpec as P

NT = 210
NF = 210


full_turn = 2.0 * math.pi


def analysis_table(freq_count):
    times_axis = jnp.arange(NT).astype(jnp.float32)
    freqs = jnp.arange(freq_count).astype(jnp.float32)
    angles = full_turn * times_axis[:, None] * freqs[None, :] / (2.0 * NF)
    return jnp.stack([jnp.cos(angles), -jnp.sin(angles)], axis=-1)


def synthesis_table():
    times_axis = jnp.arange(NT).astype(jnp.float32)
    freqs = jnp.arange(NF).astype(jnp.float32)
    angles = full_turn * freqs[:, None] * times_axis[None, :] / (2.0 * NF)
    return jnp.stack([jnp.cos(angles), -jnp.sin(angles)], axis=1)


def complex_term(left_op, right_op):
    return jnp.einsum("fpr,rfn->fpn", left_op, right_op, preferred_element_type=jnp.float32)


def per_device(hess_inverse, observations, adjoint_maps):
    highest = lax.Precision.HIGHEST
    row_count = hess_inverse.shape[0]
    sensors_dev = row_count // NT
    partial_value = lax.dot_general(
        lax.all_gather(observations, "wide", axis=0, tiled=True),
        hess_inverse,
        (((1,), (1,)), ((), ())),
        preferred_element_type=jnp.float32,
    )
    scen_total = partial_value.shape[0]
    values = partial_value.reshape(scen_total, sensors_dev, NT)
    freq_terms = jnp.einsum("nst,tfc->sfcn", values, analysis_table(NF), precision=highest)
    spectra = lax.psum_scatter(freq_terms, "narrow", scatter_dimension=1, tiled=True).astype(
        jnp.bfloat16
    )
    portion = lax.all_gather(spectra, "wide", axis=0, tiled=True)
    map_real = adjoint_maps[:, 0]
    map_imag = adjoint_maps[:, 1]
    spec_real = portion[:, :, 0]
    spec_imag = portion[:, :, 1]
    real_part = complex_term(map_real, spec_real) - complex_term(map_imag, spec_imag)
    imag_part = complex_term(map_real, spec_imag) + complex_term(map_imag, spec_real)
    real_part, imag_part = (real_part, imag_part)
    joined = jnp.stack([real_part.astype(jnp.bfloat16), imag_part.astype(jnp.bfloat16)], axis=1)
    regrouped = lax.all_to_all(joined, "narrow", split_axis=2, concat_axis=0, tiled=True)
    estimate = jnp.einsum(
        "fcpn,fct->ptn", regrouped.astype(jnp.float32), synthesis_table(), precision=highest
    )
    return estimate * (1.0 / NF)


def solution(mesh):
    return jax.shard_map(
        per_device,
        mesh=mesh,
        in_specs=(P("wide", "narrow"), P("wide", "narrow"), P("narrow", None, "wide", None)),
        out_specs=P(("wide", "narrow"), None, None),
        check_vma=False,
    )
```

profile of v0, /device:TPU:0, one launch (start us, length us, event | category | flops | bytes accessed | tf_op | source)
XLA Modules:
  0.0 171.7 jit_solution(15230354909841735653)
XLA Ops:
  0.0 25.9 %all-gather = bf16[16,1,13440]{2,1,0:T(2,128)(2,1)S(1)} all-gather(bf16[1,1,13440]{2,1,0:T(2,128)(2,1)} %bitcast.77), channel_id=1, replica_groups=mesh['wide'=16,'narrow'=2] {'wide'}, dimensions={0}, use_global_device_ids=true | all-gather | bytes 456960 | tf_op jit(solution)/shard_map/all_gather | solution.py:38
  25.9 0.0 copy-start
  25.9 18.6 %fusion.27 = f32[16,1680]{1,0:T(8,128)S(1)} fusion(bf16[1680,13440]{1,0:T(8,128)(2,1)} %param.3, bf16[16,1,13440]{2,1,0:T(2,128)(2,1)S(1)} %all-gather), kind=kOutput, calls=%fused_computation.26 | convolution fusion | flops 722534400 | bytes 45696000 | tf_op jit(solution)/shard_map/dot_general | solution.py:37
  44.6 0.1 reshape.195
  44.7 0.9 fusion.34
  45.6 0.5 convolution_bitcast_fusion
  46.1 12.3 %all-reduce.2 = bf16[8,210,2,16]{1,3,0,2:T(8,128)(2,1)S(1)} all-reduce(f32[8,210,2,16]{1,3,0,2:T(8,128)S(1)} %convolution_bitcast_fusion), channel_id=2, replica_groups=mesh['wide'=16,'narrow'=2] {'narrow'}, use_global_device_ids=true, to_apply=%region_0.0.clone | all-reduce | flops 53760 | bytes 322560
  58.4 0.0 copy-done
  58.4 0.6 dynamic-slice
  59.6 0.1 dynamic-slice_convert_fusion
  59.7 20.8 %all_gather.7 = bf16[128,105,2,16]{1,3,2,0:T(8,128)(2,1)S(1)} all-gather(bf16[8,105,2,16]{1,3,2,0:T(8,128)(2,1)S(1)} %copy.32), channel_id=1, replica_groups=mesh['wide'=16,'narrow'=2] {'wide'}, dimensions={0}, use_global_device_ids=true | all-gather | bytes 913920 | tf_op jit(solution)/shard_map/all_gather | solution.py:49
  80.5 0.2 fusion.40
  80.7 0.7 copy.49
  81.4 0.7 copy.47
  82.2 6.3 %fusion.2 = f32[105,16,384]{2,1,0:T(8,128)S(1)} fusion(bf16[105,2,384,128]{3,2,1,0:T(8,128)(2,1)} %param.5, bf16[128,105,1,16]{0,3,1,2:T(8,128)(2,1)S(1)} %copy.49), kind=kOutput, calls=%fused_computation.2 | convolution fusion | flops 165150720 | bytes 13332480 | tf_op jit(solution)/shard_map/fpr,rfn->fpn/dot_general | solution.py:30
  88.5 6.3 %fusion = f32[105,16,384]{2,1,0:T(8,128)S(1)} fusion(bf16[105,2,384,128]{3,2,1,0:T(8,128)(2,1)} %param.5, bf16[128,105,1,16]{0,3,1,2:T(8,128)(2,1)S(1)} %copy.47), kind=kOutput, calls=%fused_computation | convolution fusion | flops 165150720 | bytes 13332480 | tf_op jit(solution)/shard_map/fpr,rfn->fpn/dot_general | solution.py:30
  94.8 7.6 %fusion.17 = bf16[105,1,384,16]{2,3,0,1:T(8,128)(2,1)S(1)} fusion(f32[105,16,384]{2,1,0:T(8,128)S(1)} %fusion.2, bf16[105,2,384,128]{3,2,1,0:T(8,128)(2,1)} %param.5, bf16[128,105,1,16]{0,3,1,2:T(8,128)(2,1)S(1)} %copy.47), kind=kOutput, calls=%fused_computation.17 | convolution fusion | flops 166440960 | bytes 14622720 | tf_op jit(solution)/shard_map/fpr,rfn->fpn/dot_general | solution.py:30
  102.5 7.6 %fusion.20 = bf16[105,1,384,16]{2,3,0,1:T(8,128)(2,1)S(1)} fusion(f32[105,16,384]{2,1,0:T(8,128)S(1)} %fusion, bf16[105,2,384,128]{3,2,1,0:T(8,128)(2,1)} %param.5, bf16[128,105,1,16]{0,3,1,2:T(8,128)(2,1)S(1)} %copy.49), kind=kOutput, calls=%fused_computation.18 | convolution fusion | flops 166440960 | bytes 14622720 | tf_op jit(solution)/shard_map/fpr,rfn->fpn/dot_general | solution.py:30
  110.1 0.3 pad_maximum_fusion
  110.4 3.8 %copy.37 = bf16[105,2,384,16]{0,3,1,2:T(8,128)(2,1)} copy(bf16[105,2,384,16]{2,3,0,1:T(8,128)(2,1)S(1)} %pad_maximum_fusion) | data formatting | bytes 5160960 | tf_op jit(solution)/shard_map/stack | solution.py:57
  114.2 4.2 %all-to-all-start = ((bf16[105,2,384,16]{0,3,1,2:T(8,128)(2,1)}), bf16[105,2,384,16]{0,3,1,2:T(8,128)(2,1)S(1)}, u32[]{:S(2)}, u32[]{:S(2)}) async-start(bf16[105,2,384,16]{0,3,1,2:T(8,128)(2,1)} %copy.37), calls=%async_computation | async-start | bytes 6291456 | tf_op jit(solution)/shard_map/all_to_all | solution.py:58
  118.4 1.6 fusion.35
  120.0 35.1 %all-to-all-done = bf16[105,2,384,16]{0,3,1,2:T(8,128)(2,1)S(1)} async-done(((bf16[105,2,384,16]{0,3,1,2:T(8,128)(2,1)}), bf16[105,2,384,16]{0,3,1,2:T(8,128)(2,1)S(1)}, u32[]{:S(2)}, u32[]{:S(2)}) %all-to-all-start) | async-done | bytes 2580512 | tf_op jit(solution)/shard_map/all_to_all | solution.py:58
  155.0 4.9 %copy.39 = bf16[2,105,2,192,16]{1,0,3,2,4:T(2,128)(2,1)} copy(bf16[2,105,2,192,16]{1,4,2,3,0:T(8,128)(2,1)S(1)} %bitcast.76) | data formatting | bytes 5160960 | tf_op jit(solution)/shard_map/all_to_all | solution.py:58
  159.9 4.4 %all_to_all.16 = bf16[210,2,192,16]{0,2,1,3:T(8,128)(2,1)S(1)} reshape(bf16[2,105,2,192,16]{1,0,3,2,4:T(2,128)(2,1)} %copy.39) | data formatting | bytes 5160960 | tf_op jit(solution)/shard_map/all_to_all | solution.py:58
  164.3 3.9 %fusion.12 = f32[192,210,16]{1,0,2:T(8,128)S(1)} fusion(bf16[210,2,192,16]{0,2,1,3:T(8,128)(2,1)S(1)} %all_to_all.16, f32[210,1,210]{2,0,1:T(8,128)} %get-tuple-element.8, f32[210,1,210]{2,0,1:T(8,128)S(1)} %get-tuple-element.7), kind=kOutput, calls=%fused_computation.13 | convolution fusion | flops 3252137984 | bytes 5513760 | tf_op jit(solution)/shard_map/fcpn,fct->ptn/dot_general | solution.py:59
  168.2 3.5 %copy.40 = f32[192,210,16]{1,2,0:T(8,128)} copy(f32[192,210,16]{1,0,2:T(8,128)S(1)} %fusion.12) | data formatting | bytes 5160960 | tf_op jit(solution)/shard_map/mul | solution.py:62
  (3 shorter events, 0.0 us)
Async XLA Ops:
  25.9 32.4 %copy-start = (u32[32]{0:T(128)S(1)}, u32[32]{0:T(128)}, u32[]{:S(2)}) copy-start(u32[32]{0:T(128)} %constant.11) | copy-start | bytes 388
  114.2 40.8 %all-to-all-start = ((bf16[105,2,384,16]{0,3,1,2:T(8,128)(2,1)}), bf16[105,2,384,16]{0,3,1,2:T(8,128)(2,1)S(1)}, u32[]{:S(2)}, u32[]{:S(2)}) async-start(bf16[105,2,384,16]{0,3,1,2:T(8,128)(2,1)} %copy.37), calls=%async_computation | async-start | bytes 6291456 | tf_op jit(solution)/shard_map/all_to_all | solution.py:58
where the time goes:
time: 172 us
  blocking collectives  59 us (34%)
  matrix products  51 us (30%)
  waiting for transfers between devices  35.1 us (20%)
  local copies, waits for them, and re-layouts  19 us (11%)
  starting transfers between devices  4.17 us (2%)
  other arithmetic  2.72 us (2%)
    all_to_all x1, waiting for transfers between devices, per_device(): lax.all_to_all(joined, 'narrow', split_axis=2, concat_axis=0, tiled=True)  35.1 us
    dot_general x4, matrix products, complex_term(): jnp.einsum('fpr,rfn->fpn', left_op, right_op, preferred_element_type=jnp....  27.9 us
    all_gather x1, blocking collectives, per_device(): lax.all_gather(observations, 'wide', axis=0, tiled=True)  25.9 us
    all_gather x1, blocking collectives, per_device(): portion = lax.all_gather(spectra, 'wide', axis=0, tiled=True)  20.8 us
    dot_general x1, matrix products, per_device(): lax.dot_general(lax.all_gather(observations, 'wide', axis=0, tiled=True),...  18.6 us
    unnamed x1, blocking collectives  12.3 us
    all_to_all x2, local copies, waits for them, and re-layouts, per_device(): lax.all_to_all(joined, 'narrow', split_axis=2, concat_axis=0, tiled=True)  9.29 us
    all_to_all x1, starting transfers between devices, per_device(): lax.all_to_all(joined, 'narrow', split_axis=2, concat_axis=0, tiled=True)  4.17 us
  transfers between devices with their start and end apart: 1, of which 1 were waited for; matrix products, arithmetic and copies ran while one was open for 1% of the time, Pallas kernels for 0%

commit v1 on v0

v1 whole, which is shorter than its diff:
```python
import functools
import math

import jax
import jax.numpy as jnp
import numpy as np
from jax import lax
from jax.experimental import pallas as pl
from jax.experimental.pallas import tpu as pltpu
from jax.sharding import PartitionSpec as P

MESH = pl.DeviceIdType.MESH
LANES = 128


def angles(freqs, times, turn):
    return 2.0 * math.pi * ((freqs * times) % turn) / turn


def analysis_table(nt, nf):
    a = angles(np.arange(nt)[:, None], np.arange(nf)[None, :], 2 * nf)
    return np.stack([np.cos(a), -np.sin(a)], axis=1).astype(np.float32)


def synthesis_table(nt, nf):
    a = angles(np.arange(nf)[:, None], np.arange(nt)[None, :], 2 * nf)
    return np.stack([np.cos(a), -np.sin(a)], axis=1).astype(np.float32)


def gather_kernel(zs, x_ref, out_ref, send, recv):
    w = lax.axis_index("wide")
    z, x, c = w // 4, (w // 2) % 2, w % 2

    def at(zz, xx, cc):
        return (zz * 2 + xx) * 2 + cc

    peers = [at((z + d) % zs, x, c) for d in range(1, zs)] + [at(z, 1 - x, c), at(z, x, 1 - c)]
    barrier = pltpu.get_barrier_semaphore()
    for p in peers:
        pl.semaphore_signal(barrier, inc=1, device_id={"wide": p}, device_id_type=MESH)
    pl.semaphore_wait(barrier, len(peers))

    copies = []

    def put(src, slot, k, target):
        cp = pltpu.make_async_remote_copy(
            src_ref=src, dst_ref=out_ref.at[slot], send_sem=send.at[k], recv_sem=recv.at[k],
            device_id={"wide": target}, device_id_type=MESH)
        cp.start()
        copies.append(cp)
        return cp

    along_z = [put(x_ref, w, d - 1, at((z + d) % zs, x, c)) for d in range(1, zs)]
    base_x = zs - 1
    base_c = base_x + zs
    along_x = [put(x_ref, w, base_x, at(z, 1 - x, c))]
    along_c = [put(x_ref, w, base_c, at(z, x, 1 - c))]
    out_ref[w] = x_ref[...]
    for d in range(1, zs):
        along_z[d - 1].wait_recv()
        slot = at((z + zs - d) % zs, x, c)
        along_x.append(put(out_ref.at[slot], slot, base_x + d, at(z, 1 - x, c)))
        along_c.append(put(out_ref.at[slot], slot, base_c + d, at(z, x, 1 - c)))
    for d in range(zs):
        along_x[d].wait_recv()
        slot = at((z + zs - d) % zs, 1 - x, c)
        along_c.append(put(out_ref.at[slot], slot, base_c + zs + d, at(z, x, 1 - c)))
    for cp in along_c:
        cp.wait_recv()
    for cp in copies:
        cp.wait_send()


def gather_wide(block, wide, ident):
    zs = wide // 4
    n = zs - 1 + zs + 2 * zs
    vm = pl.BlockSpec(memory_space=pltpu.VMEM)
    return pl.pallas_call(
        functools.partial(gather_kernel, zs),
        out_shape=jax.ShapeDtypeStruct((wide,) + block.shape, block.dtype),
        in_specs=[vm], out_specs=vm,
        scratch_shapes=[pltpu.SemaphoreType.DMA((n,)), pltpu.SemaphoreType.DMA((n,))],
        compiler_params=pltpu.CompilerParams(collective_id=ident, has_side_effects=True),
        name=f"gather{ident}",
    )(block)


def map_kernel(fs, groups, half, x_ref, a_hbm, out_ref, a, m32, sent, load, send, recv):
    k = lax.axis_index("narrow")
    other = 1 - k

    def fetch(g, side, h):
        rows = pl.ds(pl.multiple_of(h * half, 64), half)
        return pltpu.make_async_copy(
            a_hbm.at[pl.ds(g * fs, fs), :, rows], a.at[pl.ds(g * fs, fs), :, rows], load.at[side, g])

    for g in range(groups):
        fetch(g, 0, other).start()
    for g in range(groups):
        fetch(g, 1, k).start()

    barrier = pltpu.get_barrier_semaphore()
    pl.semaphore_signal(barrier, inc=1, device_id={"narrow": other}, device_id_type=MESH)
    pl.semaphore_wait(barrier, 1)

    m32[...] = jnp.zeros_like(m32)
    lane = lax.broadcasted_iota(jnp.int32, (8, LANES), 1)

    def chunk(g, h, dst):
        p0 = pl.multiple_of(h * half, 64)
        for i in range(fs):
            f = g * fs + i
            parts = []
            for c in range(2):
                head = a[f, c, pl.ds(p0, 128), :]
                tail = a[f, c, pl.ds(p0 + 128, 64), :]
                parts.append(jnp.concatenate([head, tail, tail], axis=0))
            got = lax.dot_general(
                x_ref[f], jnp.concatenate(parts, axis=1), (((1,), (1,)), ((), ())),
                preferred_element_type=jnp.float32)
            for c in range(2):
                low, high = got[c * 16:c * 16 + 8], got[c * 16 + 8:c * 16 + 16]
                rows = pl.ds(c * 16 + i, 8, stride=32)
                m32[0, rows, :] = low[:, :LANES]
                m32[1, rows, :] = high[:, :LANES]
                m32[2, rows, :] = jnp.where(lane < 64, low[:, LANES:], high[:, LANES:])
        for b in range(3):
            dst[:, :, b * LANES:(b + 1) * LANES] = m32[b].reshape(8, 32, LANES).astype(jnp.bfloat16)

    def across(g):
        return pltpu.make_async_remote_copy(
            src_ref=sent.at[g], dst_ref=out_ref.at[k, g], send_sem=send.at[g], recv_sem=recv.at[g],
            device_id={"narrow": other}, device_id_type=MESH)

    def first(g, _):
        fetch(g, 0, other).wait()
        chunk(g, other, sent.at[g])

        @pl.when(g > 0)
        def _():
            across(g - 1).start()
        return 0

    lax.fori_loop(0, groups, first, 0)

    def second(g, _):
        fetch(g, 1, k).wait()
        chunk(g, k, out_ref.at[k, g])

        @pl.when(g == 0)
        def _():
            across(groups - 1).start()
        return 0

    lax.fori_loop(0, groups, second, 0)

    def drain(g, _):
        across(g).wait()
        return 0

    lax.fori_loop(0, groups, drain, 0)


def apply_maps(x, maps, fs, ident):
    nf, _, points, sensors = maps.shape
    groups, half = nf // fs, points // 2
    vm = pl.BlockSpec(memory_space=pltpu.VMEM)
    return pl.pallas_call(
        functools.partial(map_kernel, fs, groups, half),
        out_shape=jax.ShapeDtypeStruct((2, groups, 8, 32, 2 * half), jnp.bfloat16),
        in_specs=[vm, pl.BlockSpec(memory_space=pltpu.HBM)], out_specs=vm,
        scratch_shapes=[
            pltpu.VMEM(maps.shape, jnp.bfloat16),
            pltpu.VMEM((3, 8 * 32, LANES), jnp.float32),
            pltpu.VMEM((groups, 8, 32, 2 * half), jnp.bfloat16),
            pltpu.SemaphoreType.DMA((2, groups)),
            pltpu.SemaphoreType.DMA((groups,)),
            pltpu.SemaphoreType.DMA((groups,)),
        ],
        compiler_params=pltpu.CompilerParams(
            collective_id=ident, has_side_effects=True, vmem_limit_bytes=48 << 20),
        name="maps",
    )(x, maps)


def time_kernel(scale, m_ref, hi_ref, lo_ref, out_ref):
    blocks, nt = m_ref.shape[0], out_ref.shape[2]
    for j in range(8):
        m = m_ref[:, j].reshape(blocks * 32, m_ref.shape[3])
        got = lax.dot_general(m, hi_ref[...], (((0,), (0,)), ((), ())), preferred_element_type=jnp.float32)
        got += lax.dot_general(m, lo_ref[...], (((0,), (0,)), ((), ())), preferred_element_type=jnp.float32)
        got = (got * scale)[:, :nt]
        out_ref[0:128, j, :] = got[0:128]
        out_ref[0:128, j + 8, :] = got[128:256]
        out_ref[128:192, j, :] = got[256:320]
        out_ref[128:192, j + 8, :] = got[320:384]


def to_time(m, nt, nf, fs):
    blocks = m.shape[0] * m.shape[1]
    table = synthesis_table(nt, nf)
    laid = np.zeros((blocks, 2, 16, 256), np.float32)
    laid[:, :, :fs, :nt] = table.reshape(blocks, fs, 2, nt).transpose(0, 2, 1, 3)
    laid = laid.reshape(blocks * 32, 256)
    hi = laid.astype(jnp.bfloat16)
    lo = (laid - hi.astype(np.float32)).astype(jnp.bfloat16)
    vm = pl.BlockSpec(memory_space=pltpu.VMEM)
    return pl.pallas_call(
        functools.partial(time_kernel, 1.0 / nf),
        out_shape=jax.ShapeDtypeStruct((m.shape[4] // 2, 16, nt), jnp.float32),
        in_specs=[vm] * 3, out_specs=vm,
        compiler_params=pltpu.CompilerParams(vmem_limit_bytes=32 << 20),
        name="time",
    )(m.reshape((blocks,) + m.shape[2:]), jnp.asarray(hi), jnp.asarray(lo))


def per_device(wide, narrow, hess_inverse, observations, adjoint_maps):
    highest = lax.Precision.HIGHEST
    nf_dev, _, points, sensors = adjoint_maps.shape
    nf = nf_dev * narrow
    rows, cols = hess_inverse.shape
    nt = rows * wide // sensors
    scen = observations.shape[0] * wide
    sensors_dev = rows // nt
    fs = max([d for d in range(1, 17) if nf_dev % d == 0])
    tuned = (narrow == 2 and wide == 16 and scen == 16 and sensors == 128 and points == 384
             and cols % LANES == 0 and observations.shape[0] == 1)
    if tuned:
        observed = gather_wide(observations.reshape(cols // LANES, LANES), wide, 0).reshape(scen, cols)
    else:
        observed = lax.all_gather(observations, "wide", axis=0, tiled=True)
    partial_value = lax.dot_general(
        observed, hess_inverse, (((1,), (1,)), ((), ())), preferred_element_type=jnp.float32)
    values = partial_value.reshape(scen, sensors_dev, nt)
    table = jnp.asarray(analysis_table(nt, nf))
    if not tuned:
        terms = jnp.einsum("nst,tcf->sfcn", values, table, precision=highest)
        spectra = lax.psum_scatter(terms, "narrow", scatter_dimension=1, tiled=True).astype(jnp.bfloat16)
        portion = lax.all_gather(spectra, "wide", axis=0, tiled=True)
        both = portion.transpose(1, 2, 3, 0)
        re, im = both[:, 0], both[:, 1]
        x = jnp.concatenate([jnp.concatenate([re, -im], 2), jnp.concatenate([im, re], 2)], 1)
        a = adjoint_maps.transpose(0, 2, 1, 3).reshape(nf_dev, points, 2 * sensors)
        m = jnp.einsum("frk,fpk->frp", x, a, preferred_element_type=jnp.float32).astype(jnp.bfloat16)
        m = m.reshape(nf_dev, 2, scen, points)
        m = lax.all_to_all(m, "narrow", split_axis=3, concat_axis=0, tiled=True)
        est = jnp.einsum("fcnp,fct->ptn", m.astype(jnp.float32), jnp.asarray(synthesis_table(nt, nf)),
                         precision=highest)
        return est * (1.0 / nf)
    terms = jnp.einsum("nst,tcf->scnf", values, table, precision=highest)
    k = lax.axis_index("narrow")
    mine = lax.dynamic_slice_in_dim(terms, k * nf_dev, nf_dev, 3)
    theirs = lax.dynamic_slice_in_dim(terms, (1 - k) * nf_dev, nf_dev, 3)
    came = lax.ppermute(theirs.reshape(-1, nf_dev), "narrow", [(0, 1), (1, 0)])
    spectra = (mine.reshape(-1, nf_dev) + came).astype(jnp.bfloat16)
    full = gather_wide(spectra, wide, 1).reshape(sensors, 2, scen, nf_dev)
    both = full.transpose(3, 1, 2, 0)
    re, im = both[:, 0], both[:, 1]
    x = jnp.concatenate([jnp.concatenate([re, -im], 2), jnp.concatenate([im, re], 2)], 1)
    m = apply_maps(x, adjoint_maps, fs, 2)
    return to_time(m, nt, nf, fs).transpose(0, 2, 1)


def solution(mesh):
    wide, narrow = mesh.shape["wide"], mesh.shape["narrow"]
    return jax.shard_map(
        functools.partial(per_device, wide, narrow),
        mesh=mesh,
        in_specs=(P("wide", "narrow"), P("wide", "narrow"), P("narrow", None, "wide", None)),
        out_specs=P(("wide", "narrow"), None, None),
        check_vma=False,
    )
```

time: 172 us -> 147 us (0.85)
  Pallas kernels: 0 us -> 69.7 us
  blocking collectives: 59 us -> 0 us
  matrix products: 51 us -> 19.8 us
  waiting for transfers between devices: 35.1 us -> 4.2 us
  local copies, waits for them, and re-layouts: 19 us -> 48.3 us
  starting transfers between devices: 4.17 us -> 1.58 us
    pallas_call x0 -> x4, Pallas kernels: none -> 69.7 us  [the longest x1 35.5 us: apply_maps(): pl.pallas_call(functools.partial(map_kernel, fs, groups, half), out_shape...]
    all_gather x2 -> x0, blocking collectives: 46.7 us -> none  [the longest x1 25.9 us: per_device(): lax.all_gather(observations, 'wide', axis=0, tiled=True)]
    dot_general x0 -> x1, local copies, waits for them, and re-layouts: none -> 44.2 us  [per_device(): lax.dot_general(observed, hess_inverse, (((1,), (1,)), ((), ())), preferr...]
    all_to_all x1 -> x0, waiting for transfers between devices: 35.1 us -> none  [per_device(): lax.all_to_all(joined, 'narrow', split_axis=2, concat_axis=0, tiled=True)]
    dot_general x7 -> x2, matrix products: 51 us -> 19.8 us  [the longest x1 19.3 us: per_device(): lax.dot_general(observed, hess_inverse, (((1,), (1,)), ((), ())), preferr...]
    unnamed x1 -> x0, blocking collectives: 12.3 us -> none
    all_to_all x2 -> x0, local copies, waits for them, and re-layouts: 9.29 us -> none  [per_device(): lax.all_to_all(joined, 'narrow', split_axis=2, concat_axis=0, tiled=True)]
    ppermute x0 -> x1, waiting for transfers between devices: none -> 4.2 us  [per_device(): came = lax.ppermute(theirs.reshape(-1, nf_dev), 'narrow', [(0, 1), (1, 0)])]
  transfers between devices with their start and end apart: 1 -> 1, of which waited for: 1 -> 1; matrix products, arithmetic and copies ran while one was open for 1% -> 0% of each run, Pallas kernels for 0% -> 0%
where the time goes in v1:
time: 147 us; the launch traced here: 146 us
  Pallas kernels  69.7 us (47%)
  local copies, waits for them, and re-layouts  48.3 us (33%)
  matrix products  19.8 us (13%)
  waiting for transfers between devices  4.2 us (3%)
  other arithmetic  2.53 us (2%)
  starting transfers between devices  1.58 us (1%)
    dot_general x1, local copies, waits for them, and re-layouts, per_device(): lax.dot_general(observed, hess_inverse, (((1,), (1,)), ((), ())), preferr...  44.2 us
    pallas_call x1, Pallas kernels, apply_maps(): pl.pallas_call(functools.partial(map_kernel, fs, groups, half), out_shape...  35.5 us
    pallas_call x2, Pallas kernels, gather_wide(): pl.pallas_call(functools.partial(gather_kernel, zs), out_shape=jax.ShapeD...  29.7 us
    dot_general x1, matrix products, per_device(): lax.dot_general(observed, hess_inverse, (((1,), (1,)), ((), ())), preferr...  19.3 us
    pallas_call x1, Pallas kernels, to_time(): pl.pallas_call(functools.partial(time_kernel, 1.0 / nf), out_shape=jax.Sh...  4.48 us
    ppermute x1, waiting for transfers between devices, per_device(): came = lax.ppermute(theirs.reshape(-1, nf_dev), 'narrow', [(0, 1), (1, 0)])  4.2 us
  transfers between devices with their start and end apart: 1, of which 1 were waited for; matrix products, arithmetic and copies ran while one was open for 0% of the time, Pallas kernels for 0%

profile of v1, /device:TPU:0, one launch (start us, length us, event | category | flops | bytes accessed | tf_op | source)
XLA Modules:
  0.0 146.2 jit_solution(546862125964611702)
XLA Ops:
  0.0 1.6 %reduce = bf16[13440]{0:T(1024)(128)(2,1)} reduce(bf16[1,13440]{1,0:T(2,128)(2,1)} %param.7, bf16[]{:T(256)} %constant.24), dimensions={0}, to_apply=%param.7.reduce_sub_computation | reduce | bytes 53762 | tf_op args[1]
  1.6 14.5 %gather0.1 = bf16[16,105,128]{2,1,0:T(8,128)(2,1)} custom-call(bf16[105,128]{1,0:T(8,128)(2,1)} %bitcast.31), custom_call_target="tpu_custom_call" | custom-call | tf_op jit(solution)/shard_map/gather0/pallas_call | solution.py:78
  16.1 1.2 reshape.26
  17.3 44.2 %dot_general.8 = bf16[8,210,13440]{2,1,0:T(8,128)(2,1)} reshape(bf16[1680,13440]{1,0:T(8,128)(2,1)} %param.6) | data formatting | bytes 90316800 | tf_op jit(solution)/shard_map/dot_general | solution.py:232
  61.4 0.0 copy-start.2
  61.4 19.3 %convolution_bitcast_fusion = f32[16,8,210,1]{2,0,1,3:T(8,128)S(1)} fusion(bf16[16,13440,1]{1,0,2:T(8,128)(2,1)S(1)} %reshape.26, bf16[8,210,13440]{2,1,0:T(8,128)(2,1)} %dot_general.8), kind=kOutput, calls=%fused_computation.1 | convolution fusion | flops 722534400 | bytes 45696000 | tf_op jit(solution)/shard_map/dot_general | solution.py:232
  80.7 0.0 copy-done.2
  80.7 0.5 fusion.1
  81.3 0.1 dynamic-slice_bitcast_fusion.1
  81.5 1.6 %collective-permute-start = (f32[256,105]{1,0:T(8,128)S(1)}, f32[256,105]{1,0:T(8,128)S(1)}, u32[]{:S(2)}, u32[]{:S(2)}) collective-permute-start(f32[256,105]{1,0:T(8,128)S(1)} %bitcast.30), channel_id=1, source_target_pairs={{0,1},{1,0},{2,3},{3,2},{4,5},{5,4},{6,7},{7,6},{8,9},{9,8},{10,11... | collective-permute-start | bytes 322568 | tf_op jit(solution)/shard_map/ppermute | solution.py:254
  83.1 4.2 %collective-permute-done = f32[256,105]{1,0:T(8,128)S(1)} collective-permute-done((f32[256,105]{1,0:T(8,128)S(1)}, f32[256,105]{1,0:T(8,128)S(1)}, u32[]{:S(2)}, u32[]{:S(2)}) %collective-permute-start) | collective-permute-done | bytes 107552 | tf_op jit(solution)/shard_map/ppermute | solution.py:254
  87.3 0.6 fusion.x_ref
  88.0 15.2 %gather1.1 = bf16[16,256,105]{2,1,0:T(8,128)(2,1)} custom-call(bf16[256,105]{1,0:T(8,128)(2,1)} %fusion.x_ref), custom_call_target="tpu_custom_call" | custom-call | tf_op jit(solution)/shard_map/gather1/pallas_call | solution.py:78
  103.2 2.5 %copy.11 = bf16[128,2,16,105]{0,2,3,1:T(8,128)(2,1)S(1)} copy(bf16[128,2,16,105]{3,2,1,0:T(8,128)(2,1)} %bitcast.29) | data formatting | bytes 1720320 | tf_op jit(solution)/shard_map/reshape | solution.py:256
  105.7 0.1 slice_bitcast_fusion
  105.8 0.1 fusion.3
  105.9 0.3 maximum_maximum_fusion.x_ref
  106.2 0.0 copy-start
  106.2 0.0 copy-start.1
  106.2 35.5 %maps.1 = bf16[2,7,8,32,384]{4,3,2,1,0:T(8,128)(2,1)S(1)} custom-call(bf16[105,32,256]{2,1,0:T(8,128)(2,1)S(1)} %maximum_maximum_fusion.x_ref, bf16[105,2,384,128]{3,2,1,0:T(8,128)(2,1)} %a_hbm.1), custom_call_target="tpu_custom_call" | custom-call | tf_op jit(solution)/shard_map/maps/pallas_call | solution.py:168
  141.7 0.0 copy-done
  141.7 0.0 copy-done.1
  141.7 4.5 %time.1 = f32[192,16,210]{2,1,0:T(8,128)} custom-call(bf16[14,8,32,384]{3,2,1,0:T(8,128)(2,1)S(1)} %bitcast.26, bf16[448,256]{1,0:T(8,128)(2,1)S(1)} %copy-done, bf16[448,256]{1,0:T(8,128)(2,1)S(1)} %copy-done.1), custom_call_target="tpu_custom_call" | custom-call | tf_op jit(solution)/shard_map/time/pallas_call | solution.py:208
  (2 shorter events, 0.1 us)
Async XLA Ops:
  61.4 19.3 %copy-start.2 = (f32[210,2,210,1]{2,0,1,3:T(8,128)S(1)}, f32[210,2,210,1]{2,0,1,3:T(8,128)}, u32[]{:S(2)}) copy-start(f32[210,2,210,1]{2,0,1,3:T(8,128)} %constant.23) | copy-start | bytes 1058404
  81.5 5.8 %collective-permute-start = (f32[256,105]{1,0:T(8,128)S(1)}, f32[256,105]{1,0:T(8,128)S(1)}, u32[]{:S(2)}, u32[]{:S(2)}) collective-permute-start(f32[256,105]{1,0:T(8,128)S(1)} %bitcast.30), channel_id=1, source_target_pairs={{0,1},{1,0},{2,3},{3,2},{4,5},{5,4},{6,7},{7,6},{8,9},{9,8},{10,11... | collective-permute-start | bytes 322568 | tf_op jit(solution)/shard_map/ppermute | solution.py:254
  106.2 35.6 %copy-start = (bf16[448,256]{1,0:T(8,128)(2,1)S(1)}, bf16[448,256]{1,0:T(8,128)(2,1)}, u32[]{:S(2)}) copy-start(bf16[448,256]{1,0:T(8,128)(2,1)} %constant.19.clone.hi_ref) | copy-start | bytes 688132
  106.2 35.6 %copy-start.1 = (bf16[448,256]{1,0:T(8,128)(2,1)S(1)}, bf16[448,256]{1,0:T(8,128)(2,1)}, u32[]{:S(2)}) copy-start(bf16[448,256]{1,0:T(8,128)(2,1)} %constant.20.clone.lo_ref) | copy-start | bytes 688132

commit v2 on v1

--- a/solution.py
+++ b/solution.py
@@ -83,6 +83,130 @@
         compiler_params=pltpu.CompilerParams(collective_id=ident, has_side_effects=True),
         name=f"gather{ident}",
     )(block)
+
+
+def data_kernel(zs, parts, depth, obs_ref, hess_hbm, out_ref, hess, own32, mine, rows16, spread, wide_op, part, came,
+                load, send, recv, send_n, recv_n):
+    w, k = lax.axis_index("wide"), lax.axis_index("narrow")
+    z, x, c = w // 4, (w // 2) % 2, w % 2
+    step = hess.shape[0] // parts
+    blocks = mine.shape[0]
+
+    def at(zz, xx, cc):
+        return (zz * 2 + xx) * 2 + cc
+
+    def fetch(g):
+        rows = pl.ds(pl.multiple_of(g * step, 16), step)
+        return pltpu.make_async_copy(hess_hbm.at[rows], hess.at[rows], load.at[g])
+
+    for g in range(parts):
+        fetch(g).start()
+
+    peers = [at((z + d) % zs, x, c) for d in range(1, zs)] + [at(z, 1 - x, c), at(z, x, 1 - c)]
+    barrier = pltpu.get_barrier_semaphore()
+    for p in peers:
+        pl.semaphore_signal(barrier, inc=1, device_id={"wide": p}, device_id_type=MESH)
+    pl.semaphore_signal(barrier, inc=1, device_id={"narrow": 1 - k}, device_id_type=MESH)
+    for b in range(blocks):
+        own32[b:b + 1, :] = obs_ref[0:1, b * LANES:(b + 1) * LANES].astype(jnp.float32)
+    mine[...] = own32[...].astype(jnp.bfloat16)
+    pl.semaphore_wait(barrier, len(peers) + 1)
+
+    copies = []
+
+    def put(src, slot, n, target):
+        cp = pltpu.make_async_remote_copy(
+            src_ref=src, dst_ref=rows16.at[slot], send_sem=send.at[n], recv_sem=recv.at[n],
+            device_id={"wide": target}, device_id_type=MESH)
+        cp.start()
+        copies.append(cp)
+        return cp
+
+    base_x, base_c = zs - 1, 2 * zs - 1
+    along_z = [put(mine, w, d - 1, at((z + d) % zs, x, c)) for d in range(1, zs)]
+    along_x = [put(mine, w, base_x, at(z, 1 - x, c))]
+    along_c = [put(mine, w, base_c, at(z, x, 1 - c))]
+
+    def place(block, slot):
+        spread[pl.ds(slot, blocks, stride=4 * zs), :] = block.astype(jnp.float32)
+
+    place(mine[...], w)
+    for d in range(1, zs):
+        along_z[d - 1].wait_recv()
+        slot = at((z + zs - d) % zs, x, c)
+        along_x.append(put(rows16.at[slot], slot, base_x + d, at(z, 1 - x, c)))
+        along_c.append(put(rows16.at[slot], slot, base_c + d, at(z, x, 1 - c)))
+        place(rows16[slot], slot)
+    for d in range(zs):
+        along_x[d].wait_recv()
+        slot = at((z + zs - d) % zs, 1 - x, c)
+        along_c.append(put(rows16.at[slot], slot, base_c + zs + d, at(z, x, 1 - c)))
+        place(rows16[slot], slot)
+    for d in range(2 * zs):
+        along_c[d].wait_recv()
+        slot = at((z + zs - d) % zs, x, 1 - c) if d < zs else at((z + 2 * zs - d) % zs, 1 - x, 1 - c)
+        place(rows16[slot], slot)
+    scen = 4 * zs
+    for b in range(blocks):
+        wide_op[:, b * LANES:(b + 1) * LANES] = spread[b * scen:(b + 1) * scen, :].astype(jnp.bfloat16)
+
+    def across(g):
+        return pltpu.make_async_remote_copy(
+            src_ref=part.at[g], dst_ref=came.at[g], send_sem=send_n.at[g], recv_sem=recv_n.at[g],
+            device_id={"narrow": 1 - k}, device_id_type=MESH)
+
+    def product(g, _):
+        fetch(g).wait()
+        rows = pl.ds(pl.multiple_of(g * step, 16), step)
+        total = None
+        for d in range(0, wide_op.shape[1], depth):
+            term = lax.dot_general(
+                wide_op[:, d:d + depth], hess[rows, d:d + depth], (((1,), (1,)), ((), ())),
+                preferred_element_type=jnp.float32)
+            total = term if total is None else total + term
+        part[g] = total
+
+        @pl.when(g > 0)
+        def _():
+            across(g - 1).start()
+        return 0
+
+    lax.fori_loop(0, parts, product, 0)
+    for cp in copies:
+        cp.wait_send()
+    across(parts - 1).start()
+
+    def gather(g, _):
+        across(g).wait()
+        out_ref[g] = part[g] + came[g]
+        return 0
+
+    lax.fori_loop(0, parts, gather, 0)
+
+
+def data_product(observations, hess, wide, ident):
+    rows, cols = hess.shape
+    zs, blocks, parts = wide // 4, cols // LANES, 7
+    depth = LANES * max(d for d in range(1, 17) if blocks % d == 0)
+    n = zs - 1 + zs + 2 * zs
+    vm = pl.BlockSpec(memory_space=pltpu.VMEM)
+    f32, bf16, dma = jnp.float32, jnp.bfloat16, pltpu.SemaphoreType.DMA
+    shape = (parts, wide, rows // parts)
+    got = pl.pallas_call(
+        functools.partial(data_kernel, zs, parts, depth),
+        out_shape=jax.ShapeDtypeStruct(shape, f32),
+        in_specs=[vm, pl.BlockSpec(memory_space=pltpu.HBM)], out_specs=vm,
+        scratch_shapes=[
+            pltpu.VMEM((rows, cols), bf16), pltpu.VMEM((blocks, LANES), f32), pltpu.VMEM((blocks, LANES), bf16),
+            pltpu.VMEM((wide, blocks, LANES), bf16), pltpu.VMEM((wide * blocks, LANES), f32),
+            pltpu.VMEM((wide, cols), bf16), pltpu.VMEM(shape, f32), pltpu.VMEM(shape, f32),
+            dma((parts,)), dma((n,)), dma((n,)), dma((parts,)), dma((parts,)),
+        ],
+        compiler_params=pltpu.CompilerParams(
+            collective_id=ident, has_side_effects=True, vmem_limit_bytes=56 << 20),
+        name="data",
+    )(observations, hess)
+    return got.transpose(1, 0, 2).reshape(wide, rows)
 
 
 def map_kernel(fs, groups, half, x_ref, a_hbm, out_ref, a, m32, sent, load, send, recv):
@@ -224,16 +348,13 @@
     sensors_dev = rows // nt
     fs = max([d for d in range(1, 17) if nf_dev % d == 0])
     tuned = (narrow == 2 and wide == 16 and scen == 16 and sensors == 128 and points == 384
-             and cols % LANES == 0 and observations.shape[0] == 1)
-    if tuned:
-        observed = gather_wide(observations.reshape(cols // LANES, LANES), wide, 0).reshape(scen, cols)
-    else:
-        observed = lax.all_gather(observations, "wide", axis=0, tiled=True)
-    partial_value = lax.dot_general(
-        observed, hess_inverse, (((1,), (1,)), ((), ())), preferred_element_type=jnp.float32)
-    values = partial_value.reshape(scen, sensors_dev, nt)
+             and cols % LANES == 0 and observations.shape[0] == 1 and rows % 112 == 0)
     table = jnp.asarray(analysis_table(nt, nf))
     if not tuned:
+        observed = lax.all_gather(observations, "wide", axis=0, tiled=True)
+        values = lax.dot_general(
+            observed, hess_inverse, (((1,), (1,)), ((), ())), preferred_element_type=jnp.float32)
+        values = values.reshape(scen, sensors_dev, nt)
         terms = jnp.einsum("nst,tcf->sfcn", values, table, precision=highest)
         spectra = lax.psum_scatter(terms, "narrow", scatter_dimension=1, tiled=True).astype(jnp.bfloat16)
         portion = lax.all_gather(spectra, "wide", axis=0, tiled=True)
@@ -247,12 +368,10 @@
         est = jnp.einsum("fcnp,fct->ptn", m.astype(jnp.float32), jnp.asarray(synthesis_table(nt, nf)),
                          precision=highest)
         return est * (1.0 / nf)
-    terms = jnp.einsum("nst,tcf->scnf", values, table, precision=highest)
-    k = lax.axis_index("narrow")
-    mine = lax.dynamic_slice_in_dim(terms, k * nf_dev, nf_dev, 3)
-    theirs = lax.dynamic_slice_in_dim(terms, (1 - k) * nf_dev, nf_dev, 3)
-    came = lax.ppermute(theirs.reshape(-1, nf_dev), "narrow", [(0, 1), (1, 0)])
-    spectra = (mine.reshape(-1, nf_dev) + came).astype(jnp.bfloat16)
+    values = data_product(observations, hess_inverse, wide, 0).reshape(scen, sensors_dev, nt)
+    mine = lax.dynamic_slice_in_dim(table, lax.axis_index("narrow") * nf_dev, nf_dev, 2)
+    spectra = jnp.einsum("nst,tcf->scnf", values, mine, precision=highest)
+    spectra = spectra.reshape(-1, nf_dev).astype(jnp.bfloat16)
     full = gather_wide(spectra, wide, 1).reshape(sensors, 2, scen, nf_dev)
     both = full.transpose(3, 1, 2, 0)
     re, im = both[:, 0], both[:, 1]

time: 147 us -> 91.1 us (0.62)
  local copies, waits for them, and re-layouts: 48.3 us -> 4.4 us
  matrix products: 19.8 us -> 0.38 us
  Pallas kernels: 69.7 us -> 85.6 us
  waiting for transfers between devices: 4.2 us -> 0 us
  other arithmetic: 2.53 us -> 0.31 us
  starting transfers between devices: 1.58 us -> 0 us
    dot_general x1 -> x0, local copies, waits for them, and re-layouts: 44.2 us -> none  [per_device(): lax.dot_general(observed, hess_inverse, (((1,), (1,)), ((), ())), preferr...]
    pallas_call x0 -> x1, Pallas kernels: none -> 30.8 us  [data_product(): pl.pallas_call(functools.partial(data_kernel, zs, parts, depth), out_shap...]
    dot_general x2 -> x1, matrix products: 19.8 us -> 0.38 us  [per_device(): spectra = jnp.einsum('nst,tcf->scnf', values, mine, precision=highest)]
    pallas_call x2 -> x1, Pallas kernels: 29.7 us -> 15.8 us  [gather_wide(): pl.pallas_call(functools.partial(gather_kernel, zs), out_shape=jax.ShapeD...]
    ppermute x1 -> x0, waiting for transfers between devices: 4.2 us -> none  [per_device(): came = lax.ppermute(theirs.reshape(-1, nf_dev), 'narrow', [(0, 1), (1, 0)])]
    ppermute x1 -> x0, starting transfers between devices: 1.58 us -> none  [per_device(): came = lax.ppermute(theirs.reshape(-1, nf_dev), 'narrow', [(0, 1), (1, 0)])]
    unnamed x1 -> x0, other arithmetic: 1.57 us -> none
  transfers between devices with their start and end apart: 1 -> 0, of which waited for: 1 -> 0; matrix products, arithmetic and copies ran while one was open for 0% -> 0% of each run, Pallas kernels for 0% -> 0%
where the time goes in v2:
time: 91.1 us; the launch traced here: 90.8 us
  Pallas kernels  85.6 us (94%)
  local copies, waits for them, and re-layouts  4.4 us (5%)
    pallas_call x1, Pallas kernels, apply_maps(): pl.pallas_call(functools.partial(map_kernel, fs, groups, half), out_shape...  34.5 us
    pallas_call x1, Pallas kernels, data_product(): pl.pallas_call(functools.partial(data_kernel, zs, parts, depth), out_shap...  30.8 us
    pallas_call x1, Pallas kernels, gather_wide(): pl.pallas_call(functools.partial(gather_kernel, zs), out_shape=jax.ShapeD...  15.8 us
    pallas_call x1, Pallas kernels, to_time(): pl.pallas_call(functools.partial(time_kernel, 1.0 / nf), out_shape=jax.Sh...  4.47 us
    reshape x1, local copies, waits for them, and re-layouts, per_device(): full = gather_wide(spectra, wide, 1).reshape(sensors, 2, scen, nf_dev)  2.5 us

profile of v2, /device:TPU:0, one launch (start us, length us, event | category | flops | bytes accessed | tf_op | source)
XLA Modules:
  0.0 90.8 jit_solution(10027567146230381685)
XLA Ops:
  0.0 0.0 copy-start.2
  0.0 30.8 %data.1 = f32[7,16,240]{2,1,0:T(8,128)} custom-call(bf16[1,13440]{1,0:T(2,128)(2,1)} %obs_ref.1, bf16[1680,13440]{1,0:T(8,128)(2,1)} %hess_hbm.1), custom_call_target="tpu_custom_call" | custom-call | tf_op jit(solution)/shard_map/data/pallas_call | solution.py:195
  30.8 1.0 %copy.8 = f32[16,7,240]{2,1,0:T(8,128)S(1)} copy(f32[16,7,240]{2,0,1:T(8,128)} %bitcast.26) | data formatting | bytes 215040 | tf_op jit(solution)/shard_map/transpose | solution.py:209
  31.8 0.1 reshape_reshape.3
  31.9 0.0 copy-done.2
  32.0 0.4 fusion
  32.3 0.6 copy.10
  33.0 15.8 %gather1.1 = bf16[16,256,105]{2,1,0:T(8,128)(2,1)} custom-call(bf16[256,105]{1,0:T(8,128)(2,1)} %bitcast.27), custom_call_target="tpu_custom_call" | custom-call | tf_op jit(solution)/shard_map/gather1/pallas_call | solution.py:78
  48.8 2.5 %copy.11 = bf16[128,2,16,105]{0,2,3,1:T(8,128)(2,1)S(1)} copy(bf16[128,2,16,105]{3,2,1,0:T(8,128)(2,1)} %bitcast.25) | data formatting | bytes 1720320 | tf_op jit(solution)/shard_map/reshape | solution.py:375
  51.3 0.1 fusion.6
  51.4 0.1 slice_bitcast_fusion
  51.5 0.3 maximum_maximum_fusion.x_ref
  51.8 0.0 copy-start
  51.8 0.0 copy-start.1
  51.8 34.5 %maps.1 = bf16[2,7,8,32,384]{4,3,2,1,0:T(8,128)(2,1)S(1)} custom-call(bf16[105,32,256]{2,1,0:T(8,128)(2,1)S(1)} %maximum_maximum_fusion.x_ref, bf16[105,2,384,128]{3,2,1,0:T(8,128)(2,1)} %a_hbm.1), custom_call_target="tpu_custom_call" | custom-call | tf_op jit(solution)/shard_map/maps/pallas_call | solution.py:292
  86.3 0.0 copy-done
  86.4 0.0 copy-done.1
  86.4 4.5 %time.1 = f32[192,16,210]{2,1,0:T(8,128)} custom-call(bf16[14,8,32,384]{3,2,1,0:T(8,128)(2,1)S(1)} %bitcast.22, bf16[448,256]{1,0:T(8,128)(2,1)S(1)} %copy-done.1, bf16[448,256]{1,0:T(8,128)(2,1)S(1)} %copy-done), custom_call_target="tpu_custom_call" | custom-call | tf_op jit(solution)/shard_map/time/pallas_call | solution.py:332
Async XLA Ops:
  0.0 31.9 %copy-start.2 = (f32[210,2,210]{2,0,1:T(8,128)S(1)}, f32[210,2,210]{2,0,1:T(8,128)}, u32[]{:S(2)}) copy-start(f32[210,2,210]{2,0,1:T(8,128)} %constant.16.clone) | copy-start | bytes 1058404
  51.8 34.6 %copy-start = (bf16[448,256]{1,0:T(8,128)(2,1)S(1)}, bf16[448,256]{1,0:T(8,128)(2,1)}, u32[]{:S(2)}) copy-start(bf16[448,256]{1,0:T(8,128)(2,1)} %constant.18.clone.lo_ref) | copy-start | bytes 688132
  51.8 34.6 %copy-start.1 = (bf16[448,256]{1,0:T(8,128)(2,1)S(1)}, bf16[448,256]{1,0:T(8,128)(2,1)}, u32[]{:S(2)}) copy-start(bf16[448,256]{1,0:T(8,128)(2,1)} %constant.17.clone.hi_ref) | copy-start | bytes 688132

commit v3 on v2

--- a/solution.py
+++ b/solution.py
@@ -307,17 +307,30 @@
     )(x, maps)
 
 
-def time_kernel(scale, m_ref, hi_ref, lo_ref, out_ref):
-    blocks, nt = m_ref.shape[0], out_ref.shape[2]
+def time_kernel(scale, m_ref, table_ref, out_hbm, laid, sem):
+    blocks, nt = m_ref.shape[0], laid.shape[2]
+
+    def back(j, lanes):
+        m = m_ref[:, j, :, lanes].reshape(blocks * 32, lanes.stop - lanes.start)
+        got = lax.dot_general(m, table_ref[...], (((0,), (0,)), ((), ())), preferred_element_type=jnp.float32)
+        return (got * scale)[:, :nt]
+
+    def leave(n, rows):
+        return pltpu.make_async_copy(laid.at[rows], out_hbm.at[rows], sem.at[n])
+
+    first, second = leave(0, pl.ds(0, 128)), leave(1, pl.ds(128, 64))
     for j in range(8):
-        m = m_ref[:, j].reshape(blocks * 32, m_ref.shape[3])
-        got = lax.dot_general(m, hi_ref[...], (((0,), (0,)), ((), ())), preferred_element_type=jnp.float32)
-        got += lax.dot_general(m, lo_ref[...], (((0,), (0,)), ((), ())), preferred_element_type=jnp.float32)
-        got = (got * scale)[:, :nt]
-        out_ref[0:128, j, :] = got[0:128]
-        out_ref[0:128, j + 8, :] = got[128:256]
-        out_ref[128:192, j, :] = got[256:320]
-        out_ref[128:192, j + 8, :] = got[320:384]
+        got = back(j, slice(0, 256))
+        laid[0:128, j, :] = got[0:128]
+        laid[0:128, j + 8, :] = got[128:256]
+    first.start()
+    for j in range(8):
+        got = back(j, slice(256, 384))
+        laid[128:192, j, :] = got[0:64]
+        laid[128:192, j + 8, :] = got[64:128]
+    second.start()
+    first.wait()
+    second.wait()
 
 
 def to_time(m, nt, nf, fs):
@@ -326,16 +339,16 @@
     laid = np.zeros((blocks, 2, 16, 256), np.float32)
     laid[:, :, :fs, :nt] = table.reshape(blocks, fs, 2, nt).transpose(0, 2, 1, 3)
     laid = laid.reshape(blocks * 32, 256)
-    hi = laid.astype(jnp.bfloat16)
-    lo = (laid - hi.astype(np.float32)).astype(jnp.bfloat16)
+    laid = laid.astype(jnp.bfloat16)
     vm = pl.BlockSpec(memory_space=pltpu.VMEM)
     return pl.pallas_call(
         functools.partial(time_kernel, 1.0 / nf),
         out_shape=jax.ShapeDtypeStruct((m.shape[4] // 2, 16, nt), jnp.float32),
-        in_specs=[vm] * 3, out_specs=vm,
+        in_specs=[vm] * 2, out_specs=pl.BlockSpec(memory_space=pltpu.HBM),
+        scratch_shapes=[pltpu.VMEM((m.shape[4] // 2, 16, nt), jnp.float32), pltpu.SemaphoreType.DMA((2,))],
         compiler_params=pltpu.CompilerParams(vmem_limit_bytes=32 << 20),
         name="time",
-    )(m.reshape((blocks,) + m.shape[2:]), jnp.asarray(hi), jnp.asarray(lo))
+    )(m.reshape((blocks,) + m.shape[2:]), jnp.asarray(laid))
 
 
 def per_device(wide, narrow, hess_inverse, observations, adjoint_maps):

time: 91.1 us -> 89.6 us (0.984)
  Pallas kernels: 85.6 us -> 84.2 us
    pallas_call x1, Pallas kernels: 4.47 us -> 3.03 us  [to_time(): pl.pallas_call(functools.partial(time_kernel, 1.0 / nf), out_shape=jax.Sh...]
where the time goes in v3:
time: 89.6 us; the launch traced here: 89.4 us
  Pallas kernels  84.2 us (94%)
  local copies, waits for them, and re-layouts  4.4 us (5%)
    pallas_call x1, Pallas kernels, apply_maps(): pl.pallas_call(functools.partial(map_kernel, fs, groups, half), out_shape...  34.5 us
    pallas_call x1, Pallas kernels, data_product(): pl.pallas_call(functools.partial(data_kernel, zs, parts, depth), out_shap...  30.8 us
    pallas_call x1, Pallas kernels, gather_wide(): pl.pallas_call(functools.partial(gather_kernel, zs), out_shape=jax.ShapeD...  15.8 us
    pallas_call x1, Pallas kernels, to_time(): pl.pallas_call(functools.partial(time_kernel, 1.0 / nf), out_shape=jax.Sh...  3.03 us
    reshape x1, local copies, waits for them, and re-layouts, per_device(): full = gather_wide(spectra, wide, 1).reshape(sensors, 2, scen, nf_dev)  2.5 us

profile of v3, /device:TPU:0, one launch (start us, length us, event | category | flops | bytes accessed | tf_op | source)
XLA Modules:
  0.0 89.4 jit_solution(13378394867832097845)
XLA Ops:
  0.0 0.0 copy-start.1
  0.0 30.8 %data.1 = f32[7,16,240]{2,1,0:T(8,128)} custom-call(bf16[1,13440]{1,0:T(2,128)(2,1)} %obs_ref.1, bf16[1680,13440]{1,0:T(8,128)(2,1)} %hess_hbm.1), custom_call_target="tpu_custom_call" | custom-call | tf_op jit(solution)/shard_map/data/pallas_call | solution.py:195
  30.8 1.0 %copy.7 = f32[16,7,240]{2,1,0:T(8,128)S(1)} copy(f32[16,7,240]{2,0,1:T(8,128)} %bitcast.26) | data formatting | bytes 215040 | tf_op jit(solution)/shard_map/transpose | solution.py:209
  31.8 0.1 reshape_reshape.3
  31.9 0.0 copy-done.1
  31.9 0.4 fusion
  32.3 0.6 copy.9
  33.0 15.8 %gather1.1 = bf16[16,256,105]{2,1,0:T(8,128)(2,1)} custom-call(bf16[256,105]{1,0:T(8,128)(2,1)} %bitcast.27), custom_call_target="tpu_custom_call" | custom-call | tf_op jit(solution)/shard_map/gather1/pallas_call | solution.py:78
  48.8 2.5 %copy.10 = bf16[128,2,16,105]{0,2,3,1:T(8,128)(2,1)S(1)} copy(bf16[128,2,16,105]{3,2,1,0:T(8,128)(2,1)} %bitcast.25) | data formatting | bytes 1720320 | tf_op jit(solution)/shard_map/reshape | solution.py:388
  51.3 0.1 fusion.6
  51.4 0.1 slice_bitcast_fusion
  51.5 0.3 maximum_maximum_fusion.x_ref
  51.8 0.0 copy-start
  51.8 34.5 %maps.1 = bf16[2,7,8,32,384]{4,3,2,1,0:T(8,128)(2,1)S(1)} custom-call(bf16[105,32,256]{2,1,0:T(8,128)(2,1)S(1)} %maximum_maximum_fusion.x_ref, bf16[105,2,384,128]{3,2,1,0:T(8,128)(2,1)} %a_hbm.1), custom_call_target="tpu_custom_call" | custom-call | tf_op jit(solution)/shard_map/maps/pallas_call | solution.py:292
  86.3 0.0 copy-done
  86.3 3.0 %time.1 = f32[192,16,210]{2,1,0:T(8,128)} custom-call(bf16[14,8,32,384]{3,2,1,0:T(8,128)(2,1)S(1)} %bitcast.22, bf16[448,256]{1,0:T(8,128)(2,1)S(1)} %copy-done), custom_call_target="tpu_custom_call" | custom-call | tf_op jit(solution)/shard_map/time/pallas_call | solution.py:344
Async XLA Ops:
  0.0 31.9 %copy-start.1 = (f32[210,2,210]{2,0,1:T(8,128)S(1)}, f32[210,2,210]{2,0,1:T(8,128)}, u32[]{:S(2)}) copy-start(f32[210,2,210]{2,0,1:T(8,128)} %constant.14.clone) | copy-start | bytes 1058404
  51.8 34.5 %copy-start = (bf16[448,256]{1,0:T(8,128)(2,1)S(1)}, bf16[448,256]{1,0:T(8,128)(2,1)}, u32[]{:S(2)}) copy-start(bf16[448,256]{1,0:T(8,128)(2,1)} %constant.15.clone.table_ref) | copy-start | bytes 688132
